TPU v7x, 32 devices: a whole 2x2x4 slice. The times are simulated.
32 devices in a mesh: group: 2 (over x), tp: 16 (over z, y, core).
Axes of the slice: x: 2, y: 2, z: 4, core: 2. Of those that a mesh axis runs over, the one named last changes fastest.
Arguments:
- hidden_states: bfloat16 [16, 2, 8192], P('group'), parts along dimension 0, may hold values from -6 to 6
- qkv_weight: bfloat16 [10240, 8192], P('tp'), may hold values from -0.0625 to 0.0625
- out_weight: bfloat16 [8192, 8192], P('tp'), may hold values from -0.0625 to 0.0625
- cache_pages: bfloat16 [2048, 128, 256], P(('group', 'tp')), parts along dimension 0, may hold values from -6 to 6
- context_lengths: int32 [16], P('group'), parts along dimension 0, may hold values from 1 to 2046, 8184 in all
- new_units: int32 [128], P('group'), parts along dimension 0, may hold values from 0 to 63, as said below
- old_pages: int32 [2048], P('group'), parts along dimension 0, may hold values from 0 to 1023, as said below
Outputs:
- mixed_out: bfloat16 [16, 2, 8192], P('group', None, 'tp'), parts along dimension 0
- cache_out: bfloat16 [2048, 128, 256], P(('group', 'tp')), parts along dimension 0
There are 2 independent parts, one for each index of `group`. A program takes and returns all parts, laid end to end along the dimension named above; an argument that names none is the same for every part. Nothing has to cross between parts.
Inputs may be any that keep to these rules, and one draw needn't show every extreme that they name: `new_units`: A permutation of all request head groups; slot q of the new layout is on device q // 4. `old_pages`: A permutation of all logical pages (page u * 16 + i is page i of unit u); position p is on device p // 64. The pages that one device holds go to exactly 16 devices of the new layout, exactly 4 to each.
All inputs are finite; a program needn't handle non-finite values.
Results may differ from a plain program's by a relative error of at most 0.013.
Values may be sent and summed in bfloat16 or wider, within the bound.
A program may use at most 128 MiB of HBM per device.

v0:
```python
import math

import jax
import jax.numpy as jnp
from jax import lax
from jax.sharding import PartitionSpec as P

D = 8192
HEADS = 64
KVH = 8
HD = 128
U_DEV = 4
MAXCTX = 2048
PAGE = 128


rope_base = 10000.0


def rotate_positions(values, positions):
    half_dim = values.shape[-1] // 2
    frequency = rope_base ** (-(jnp.arange(half_dim, dtype=jnp.float32) * 2.0 / values.shape[-1]))
    angles = positions.astype(jnp.float32)[..., None] * frequency
    cosine = jnp.concatenate([jnp.cos(angles), jnp.cos(angles)], axis=-1)
    sine_table = jnp.concatenate([jnp.sin(angles), jnp.sin(angles)], axis=-1)
    turned = jnp.concatenate([-values[..., half_dim:], values[..., :half_dim]], axis=-1)
    return values * cosine + turned * sine_table


def prepare(unit_qkv, base_lengths):
    group_count = HEADS // KVH
    count_units = unit_qkv.shape[0]
    positions = base_lengths[:, None] + jnp.arange(2, dtype=jnp.int32)[None, :]
    widened = unit_qkv.astype(jnp.float32)
    queries = widened[..., : group_count * HD].reshape(count_units, 2, group_count, HD)
    queries = rotate_positions(queries, positions[:, :, None]).astype(jnp.bfloat16)
    new_keys = rotate_positions(
        widened[..., group_count * HD : (group_count + 1) * HD], positions
    ).astype(jnp.bfloat16)
    new_values = unit_qkv[..., (group_count + 1) * HD :]
    return (queries, new_keys, new_values)


def context_terms(context, queries, valid_count):
    score_scale = 1.0 / math.sqrt(HD)
    cached_keys = context[..., :HD]
    cached_values = context[..., HD:]
    scores = (
        jnp.einsum("psgd,ptd->psgt", queries, cached_keys, preferred_element_type=jnp.float32)
        * score_scale
    )
    visible = jnp.arange(context.shape[1], dtype=jnp.int32)[None, :] < valid_count[:, None]
    weights = jnp.where(visible[:, None, None, :], jnp.exp(scores), 0.0)
    totals = jnp.sum(weights, axis=-1)
    weighted = jnp.einsum(
        "psgt,ptd->psgd",
        weights.astype(jnp.bfloat16),
        cached_values,
        preferred_element_type=jnp.float32,
    )
    return (weighted, totals)


def own_terms(queries, new_keys, new_values):
    score_scale = 1.0 / math.sqrt(HD)
    scores = (
        jnp.einsum("usgd,ujd->usgj", queries, new_keys, preferred_element_type=jnp.float32)
        * score_scale
    )
    recent = jnp.arange(2, dtype=jnp.int32)[None, :] <= jnp.arange(2, dtype=jnp.int32)[:, None]
    weights = jnp.where(recent[None, :, None, :], jnp.exp(scores), 0.0)
    totals = jnp.sum(weights, axis=-1)
    weighted = jnp.einsum(
        "usgj,ujd->usgd",
        weights.astype(jnp.bfloat16),
        new_values,
        preferred_element_type=jnp.float32,
    )
    return (weighted, totals)


def body(hidden_states, qkv_weight, out_weight, cache_pages, context_lengths, new_units, old_pages):
    devices = lax.axis_size("tp")
    device = lax.axis_index("tp")
    requests = hidden_states.shape[0]
    rows_dev = qkv_weight.shape[0]
    pages_dev, page_rows, page_width = cache_pages.shape
    group_count = HEADS // KVH
    unit_rows = (group_count + 2) * HD
    per_unit = MAXCTX // PAGE
    unit_slots = U_DEV
    capacity = max(1, pages_dev // devices)
    total_units = new_units.shape[0]
    total_pages = old_pages.shape[0]
    flat_rows = hidden_states.reshape(requests * 2, D)
    partial_qkv = lax.dot_general(
        flat_rows, qkv_weight, (((1,), (1,)), ((), ())), preferred_element_type=jnp.float32
    )
    partial_qkv = partial_qkv.astype(jnp.bfloat16).reshape(requests, 2, rows_dev)
    slot_index = (
        jnp.zeros((total_units,), jnp.int32)
        .at[new_units]
        .set(jnp.arange(total_units, dtype=jnp.int32))
    )
    own_units = lax.dynamic_slice_in_dim(new_units, device * unit_slots, unit_slots)
    own_requests = own_units // KVH
    own_heads = own_units % KVH
    own_lengths = context_lengths[own_requests]
    local_ids = lax.dynamic_slice_in_dim(old_pages, device * pages_dev, pages_dev)
    local_units = local_ids // per_unit
    local_index = local_ids % per_unit
    target_dev = (slot_index[local_units] * per_unit + local_index) // pages_dev
    local_order = jnp.arange(pages_dev, dtype=jnp.int32)
    send_rank = jnp.sum(
        (
            (target_dev[:, None] == target_dev[None, :])
            & (local_order[None, :] < local_order[:, None])
        ).astype(jnp.int32),
        axis=1,
    )
    outgoing = (
        jnp.zeros((devices, capacity, page_rows, page_width), jnp.bfloat16)
        .at[target_dev, send_rank]
        .set(cache_pages)
    )
    arrived = lax.all_to_all(outgoing, "tp", split_axis=0, concat_axis=0, tiled=True)
    stored_position = (
        jnp.zeros((total_pages,), jnp.int32)
        .at[old_pages]
        .set(jnp.arange(total_pages, dtype=jnp.int32))
    )
    wanted = (
        own_units[:, None] * per_unit + jnp.arange(per_unit, dtype=jnp.int32)[None, :]
    ).reshape(pages_dev)
    source_pos = stored_position[wanted]
    source_dev = source_pos // pages_dev
    source_slot = source_pos % pages_dev
    arrival_rank = jnp.sum(
        (
            (source_dev[:, None] == source_dev[None, :])
            & (source_slot[None, :] < source_slot[:, None])
        ).astype(jnp.int32),
        axis=1,
    )
    relaid = arrived[source_dev, arrival_rank]
    contexts = relaid.reshape(unit_slots, MAXCTX, page_width)
    sources_per_head = unit_rows // rows_dev
    request_table = (new_units // KVH).reshape(devices, unit_slots)
    outgoing_rows = partial_qkv[request_table]
    incoming = lax.all_to_all(outgoing_rows, "tp", split_axis=0, concat_axis=0, tiled=True)
    grouped = jnp.moveaxis(incoming.reshape(KVH, sources_per_head, unit_slots, 2, rows_dev), 2, 0)
    chosen = jnp.take_along_axis(grouped, own_heads[:, None, None, None, None], axis=1)[:, 0]
    own_rows = chosen.transpose(0, 2, 1, 3).reshape(unit_slots, 2, unit_rows)
    queries, new_keys, new_values = prepare(own_rows, own_lengths)
    cache_sums, cache_totals = context_terms(contexts, queries, own_lengths)
    own_sums, own_totals = own_terms(queries, new_keys, new_values)
    attended = ((cache_sums + own_sums) / (cache_totals + own_totals)[..., None]).astype(
        jnp.bfloat16
    )
    attended = attended.reshape(unit_slots, 2, group_count * HD)
    all_heads = lax.all_gather(attended, "tp", axis=0, tiled=True)
    logical = (
        all_heads[slot_index]
        .reshape(requests, KVH, 2, group_count * HD)
        .transpose(0, 2, 1, 3)
        .reshape(requests * 2, HEADS * HD)
    )
    mixed_rows = lax.dot_general(
        logical, out_weight, (((1,), (1,)), ((), ())), preferred_element_type=jnp.float32
    )
    mixed_rows = mixed_rows.astype(jnp.bfloat16).reshape(requests, 2, out_weight.shape[0])
    fresh_rows = jnp.concatenate([new_keys, new_values], axis=-1)
    positions = jnp.arange(MAXCTX, dtype=jnp.int32)[None, :]
    contexts = jnp.where(
        (positions == own_lengths[:, None])[..., None], fresh_rows[:, 0:1], contexts
    )
    contexts = jnp.where(
        (positions == own_lengths[:, None] + 1)[..., None], fresh_rows[:, 1:2], contexts
    )
    return (mixed_rows, contexts.reshape(pages_dev, page_rows, page_width))


def solution(mesh):
    in_specs = (
        P("group", None, None),
        P("tp", None),
        P("tp", None),
        P(("group", "tp"), None, None),
        P("group"),
        P("group"),
        P("group"),
    )
    out_specs = (P("group", None, "tp"), P(("group", "tp"), None, None))
    return jax.shard_map(body, mesh=mesh, in_specs=in_specs, out_specs=out_specs, check_vma=False)
```

profile of v0, /device:TPU:1, one launch (start us, length us, event | category | flops | bytes accessed | tf_op | source)
XLA Modules:
  0.0 179.7 jit_solution(12315859373717689695)
XLA Ops:
  0.6 0.7 and_select_fusion.6
  1.3 1.0 reshape.412
  2.4 6.8 %convolution_convert_fusion = bf16[16,640]{1,0:T(8,128)(2,1)S(1)} fusion(bf16[16,8192]{1,0:T(8,128)(2,1)S(1)} %reshape.412, bf16[640,8192]{1,0:T(8,128)(2,1)} %param.8), kind=kOutput, calls=%fused_computation.19 | convolution fusion | flops 167782400 | bytes 10768384 | tf_op jit(solution)/shard_map/dot_general | solution.py:96
  9.2 0.1 reshape.414
  9.3 0.1 reshape.434
  9.4 1.5 gather_fusion.1
  11.0 7.3 %all-to-all-start = ((bf16[16,4,2,640]{3,2,1,0:T(2,128)(2,1)}), bf16[16,4,2,640]{3,2,1,0:T(2,128)(2,1)S(1)}, u32[]{:S(2)}, u32[]{:S(2)}) async-start(bf16[16,4,2,640]{3,2,1,0:T(2,128)(2,1)} %bitcast), calls=%async_computation | async-start | bytes 327680 | tf_op jit(solution)/shard_map/all_to_all | solution.py:150
  18.3 0.1 compare_select_fusion.8
  18.4 0.8 scatter_custom_fusion
  19.2 0.8 gather_fusion.2
  20.0 0.2 convert_reduce_fusion.1
  20.2 2.5 %broadcast_in_dim.130 = bf16[16,4,128,256]{3,2,1,0:T(8,128)(2,1)} broadcast(bf16[]{:T(256)} %constant.132.clone.1), dimensions={} | broadcast | bytes 4194306 | tf_op jit(solution)/shard_map/broadcast_in_dim | solution.py:122
  22.7 12.5 %scatter_fusion = bf16[16,4,128,256]{3,2,1,0:T(8,128)(2,1)} fusion(bf16[16,4,128,256]{3,2,1,0:T(8,128)(2,1)} %broadcast_in_dim.130, s32[64]{0:T(128)S(1)} %fusion.28, bf16[64,128,256]{2,1,0:T(8,128)(2,1)} %param.10), kind=kCustom, calls=%fused_computation.8 | custom fusion | bytes 12583424 | tf_op jit(solution)/shard_map/scatter | solution.py:124
  35.2 6.2 %all-to-all-start.1 = ((bf16[16,4,128,256]{3,2,1,0:T(8,128)(2,1)}), bf16[16,4,128,256]{3,2,1,0:T(8,128)(2,1)}, u32[]{:S(2)}, u32[]{:S(2)}) async-start(bf16[16,4,128,256]{3,2,1,0:T(8,128)(2,1)} %scatter_fusion), calls=%async_computation.1 | async-start | bytes 8388608 | tf_op jit(solution)/shard_map/all_to_all | solution.py:126
  41.3 0.1 compare_select_fusion.10
  41.4 0.1 iota_add_fusion
  41.5 0.1 add.228
  41.6 0.6 gather_fusion
  42.2 0.1 eq.69
  42.3 0.1 eq.70
  42.5 0.1 lt.205
  42.6 4.3 %scatter_custom_fusion.2 = s32[1024]{0:T(1024)S(1)} fusion(s32[1024]{0:T(1024)S(1)} %compare_select_fusion.1, s32[1024]{0:T(1024)S(1)} %iota.73, s32[]{:T(128)} %constant.122.clone.1), kind=kCustom, calls=%fused_computation.75 | custom fusion | bytes 4100 | tf_op jit(solution)/shard_map/scatter | solution.py:130
  46.9 0.7 gather_fusion.3
  47.6 0.1 bitcast_compare_fusion.1
  47.8 0.1 add_convert_fusion
  47.9 0.1 multiply_cosine_fusion.1
  48.1 0.1 maximum_bitcast_fusion
  48.2 0.2 convert_reduce_fusion
  48.4 0.1 iota_compare_fusion.1
  48.5 0.1 copy.18
  48.6 0.6 gather_fusion.6
  49.2 0.1 broadcast_select_fusion
  49.4 0.1 multiply_sine_fusion
  49.5 0.1 fusion.12
  49.7 0.1 slice_negate_fusion
  49.7 0.1 fusion.9
  49.8 0.2 fusion.33
  50.0 69.4 %all-to-all-done.1 = bf16[16,4,128,256]{3,2,1,0:T(8,128)(2,1)} async-done(((bf16[16,4,128,256]{3,2,1,0:T(8,128)(2,1)}), bf16[16,4,128,256]{3,2,1,0:T(8,128)(2,1)}, u32[]{:S(2)}, u32[]{:S(2)}) %all-to-all-start.1) | async-done | bytes 4194336 | tf_op jit(solution)/shard_map/all_to_all | solution.py:126
  119.5 5.0 %gather_fusion.4 = bf16[64,128,256]{2,1,0:T(8,128)(2,1)} fusion(bf16[16,4,128,256]{3,2,1,0:T(8,128)(2,1)} %all-to-all-done.1, s32[64]{0:T(128)S(1)} %fusion.27), kind=kCustom, calls=%fused_computation.4 | custom fusion | bytes 8389120 | tf_op jit(solution)/shard_map/gather | solution.py:145
  124.5 2.3 %fusion.32 = (f32[4,2,8]{2,1,0:T(2,128)S(1)}, bf16[4,2,8,2048]{3,2,1,0:T(8,128)(2,1)S(1)}) fusion(bf16[4,2,8,128]{3,2,1,0:T(8,128)(2,1)S(1)} %fusion.9, bf16[4,2048,256]{2,1,0:T(8,128)(2,1)} %bitcast.104, pred[4,2048]{1,0:T(4,128)(4,1)S(1)} %iota_compare_fusion.1), kind=kOutput, calls=%fused_computation.131 | convolution fusion | flops 34078656 | bytes 2384128 | tf_op jit(solution)/shard_map/psgd,ptd->psgt/dot_general | solution.py:49
  126.8 2.0 %fusion.2 = f32[4,2,8,128]{3,2,1,0:T(8,128)S(1)} fusion(bf16[4,2048,256]{2,1,0:T(8,128)(2,1)} %bitcast.105, bf16[4,2,8,2048]{3,2,1,0:T(8,128)(2,1)S(1)} %get-tuple-element.24), kind=kOutput, calls=%fused_computation.15 | convolution fusion | flops 33554432 | bytes 2392064 | tf_op jit(solution)/shard_map/psgt,ptd->psgd/dot_general | solution.py:55
  128.8 0.2 fusion.4
  129.0 35.4 %all_gather.3 = bf16[64,2,1024]{2,1,0:T(2,128)(2,1)S(1)} all-gather(bf16[4,2,1024]{2,1,0:T(2,128)(2,1)S(1)} %reshape.420), channel_id=1, replica_groups=mesh['group'=2,'tp'=16] {'tp'}, dimensions={0}, use_global_device_ids=true | all-gather | bytes 278528 | tf_op jit(solution)/shard_map/all_gather | solution.py:161
  164.5 1.1 gather_fusion.5
  165.7 0.2 copy.27
  165.8 5.6 %convolution_convert_fusion.1 = bf16[16,512]{1,0:T(8,128)(2,1)S(1)} fusion(bf16[16,8192]{1,0:T(8,128)(2,1)S(1)} %bitcast.106, bf16[512,8192]{1,0:T(8,128)(2,1)} %param.9), kind=kOutput, calls=%fused_computation.21 | convolution fusion | flops 134225920 | bytes 8667136 | tf_op jit(solution)/shard_map/dot_general | solution.py:168
  171.5 0.6 reshape.423
  172.1 7.6 %select_select_fusion = bf16[64,128,256]{2,1,0:T(8,128)(2,1)} fusion(bf16[64,128,256]{2,1,0:T(8,128)(2,1)} %gather_fusion.4, pred[64,128]{1,0:T(8,128)(4,1)S(1)} %get-tuple-element.11, pred[64,128]{1,0:T(8,128)(4,1)S(1)} %get-tuple-element.10, bf16[64,256]{1,0:T(8,128)(2,1)S(1)} %bitcast.115, bf16[64,256]{1,0:T(8,128)(2,1)S(1)} %bitcast.116), kind=kLoop, calls=%fused_computation.10 | loop fusion | flops 4194304 | bytes 8470528 | tf_op jit(solution)/shard_map/jit(_where)/select_n | solution.py:177
  (46 shorter events, 0.5 us)
Async XLA Ops:
  0.6 41.0 %copy-start = (s32[8]{0:T(128)S(1)}, s32[8]{0:T(128)}, u32[]{:S(2)}) copy-start(s32[8]{0:T(128)} %param.11) | copy-start | bytes 100
  2.4 15.9 %copy-start.1 = (s32[1024]{0:T(1024)S(1)}, s32[1024]{0:T(1024)}, u32[]{:S(2)}) copy-start(s32[1024]{0:T(1024)} %param.13) | copy-start | bytes 12292
  11.0 24.2 %all-to-all-start = ((bf16[16,4,2,640]{3,2,1,0:T(2,128)(2,1)}), bf16[16,4,2,640]{3,2,1,0:T(2,128)(2,1)S(1)}, u32[]{:S(2)}, u32[]{:S(2)}) async-start(bf16[16,4,2,640]{3,2,1,0:T(2,128)(2,1)} %bitcast), calls=%async_computation | async-start | bytes 327680 | tf_op jit(solution)/shard_map/all_to_all | solution.py:150
  35.2 6.2 %copy-start.2 = (s32[64]{0:T(128)S(1)}, s32[64]{0:T(128)}, u32[]{:S(2)}) copy-start(s32[64]{0:T(128)} %param.12) | copy-start | bytes 772
  35.2 84.3 %all-to-all-start.1 = ((bf16[16,4,128,256]{3,2,1,0:T(8,128)(2,1)}), bf16[16,4,128,256]{3,2,1,0:T(8,128)(2,1)}, u32[]{:S(2)}, u32[]{:S(2)}) async-start(bf16[16,4,128,256]{3,2,1,0:T(8,128)(2,1)} %scatter_fusion), calls=%async_computation.1 | async-start | bytes 8388608 | tf_op jit(solution)/shard_map/all_to_all | solution.py:126
where the time goes:
time: 181 us; the launch traced here: 180 us
  waiting for transfers between devices  69.4 us (38%)
  blocking collectives  35.4 us (20%)
  local copies, waits for them, and re-layouts  33.2 us (18%)
  matrix products  17.2 us (10%)
  starting transfers between devices  13.5 us (7%)
  other arithmetic  10 us (6%)
    all_to_all x1, waiting for transfers between devices, body(): lax.all_to_all(outgoing, 'tp', split_axis=0, concat_axis=0, tiled=True)  69.4 us
    all_gather x1, blocking collectives, body(): all_heads = lax.all_gather(attended, 'tp', axis=0, tiled=True)  35.4 us
    scatter x1, local copies, waits for them, and re-layouts, body(): outgoing = jnp.zeros((devices, capacity, page_rows, page_width), jnp.bflo...  12.5 us
    select_n x1, other arithmetic, body(): jnp.where((positions == own_lengths[:, None] + 1)[..., None], fresh_rows[...  7.63 us
    all_to_all x1, starting transfers between devices, body(): lax.all_to_all(outgoing_rows, 'tp', split_axis=0, concat_axis=0, tiled=True)  7.34 us
    dot_general x1, matrix products, body(): lax.dot_general(flat_rows, qkv_weight, (((1,), (1,)), ((), ())), preferre...  6.81 us
    all_to_all x1, starting transfers between devices, body(): lax.all_to_all(outgoing, 'tp', split_axis=0, concat_axis=0, tiled=True)  6.15 us
    dot_general x1, matrix products, body(): lax.dot_general(logical, out_weight, (((1,), (1,)), ((), ())), preferred_...  5.64 us
  transfers between devices with their start and end apart: 2, of which 1 were waited for; matrix products, arithmetic and copies ran while one was open for 14% of the time, Pallas kernels for 0%

commit v1 on v0

--- a/solution.py
+++ b/solution.py
@@ -3,6 +3,8 @@
 import jax
 import jax.numpy as jnp
 from jax import lax
+from jax.experimental import pallas as pl
+from jax.experimental.pallas import tpu as pltpu
 from jax.sharding import PartitionSpec as P
 
 D = 8192
@@ -79,7 +81,7 @@
     return (weighted, totals)
 
 
-def body(hidden_states, qkv_weight, out_weight, cache_pages, context_lengths, new_units, old_pages):
+def plain_body(hidden_states, qkv_weight, out_weight, cache_pages, context_lengths, new_units, old_pages):
     devices = lax.axis_size("tp")
     device = lax.axis_index("tp")
     requests = hidden_states.shape[0]
@@ -180,6 +182,473 @@
     return (mixed_rows, contexts.reshape(pages_dev, page_rows, page_width))
 
 
+def index_tables(context_lengths, new_units, old_pages, pages_dev):
+    device = lax.axis_index("tp")
+    per_unit = MAXCTX // PAGE
+    total_units = new_units.shape[0]
+    total_pages = old_pages.shape[0]
+    capacity = pages_dev // lax.axis_size("tp")
+    places = jnp.arange(pages_dev, dtype=jnp.int32)
+    slots = jnp.arange(total_units, dtype=jnp.int32)
+
+    def pick(hit, values):
+        return jnp.sum(jnp.where(hit, values[None, :], 0), axis=1)
+
+    def ranks(owner, order):
+        before = (owner[:, None] == owner[None, :]) & (order[None, :] < order[:, None])
+        return jnp.sum(before.astype(jnp.int32), axis=1)
+
+    local_ids = lax.dynamic_slice_in_dim(old_pages, device * pages_dev, pages_dev)
+    target_slot = pick((local_ids // per_unit)[:, None] == new_units[None, :], slots)
+    target_dev = target_slot // U_DEV
+    sent_at = target_dev * capacity + ranks(target_dev, places)
+    sent = places[:, None] == sent_at[None, :]
+    send_order = pick(sent, places)
+    send_ids = pick(sent, local_ids)
+    own_units = lax.dynamic_slice_in_dim(new_units, device * U_DEV, U_DEV)
+    wanted = (
+        own_units[:, None] * per_unit + jnp.arange(per_unit, dtype=jnp.int32)[None, :]
+    ).reshape(pages_dev)
+    source_pos = pick(
+        wanted[:, None] == old_pages[None, :], jnp.arange(total_pages, dtype=jnp.int32)
+    )
+    source_dev = source_pos // pages_dev
+    arrives_at = source_dev * capacity + ranks(source_dev, source_pos)
+    arrival_slot = pick(places[:, None] == arrives_at[None, :], places // per_unit)
+    slot_of_unit = pick(slots[:, None] == new_units[None, :], slots)
+    requests = context_lengths.shape[0]
+    send_units = send_ids // per_unit
+    send_lengths = pick(
+        (send_units // KVH)[:, None] == jnp.arange(requests, dtype=jnp.int32)[None, :],
+        context_lengths,
+    )
+    send_left = send_lengths - (send_ids % per_unit) * PAGE
+    send_query = (send_units % KVH) * requests + send_units // KVH
+    own_heads, own_requests = own_units % KVH, own_units // KVH
+    table = jnp.concatenate(
+        [
+            send_query, send_left, arrival_slot, slot_of_unit,
+            own_heads * requests + own_requests, own_heads, own_requests,
+        ]
+    )
+    return send_order, arrives_at, table
+
+
+def sort_kernel(order_ref, pages_ref, out_ref, buf, in_sem, out_sem):
+    count = buf.shape[0]
+
+    def inward(i):
+        return pltpu.make_async_copy(pages_ref.at[order_ref[i]], buf.at[i], in_sem.at[i])
+
+    def outward(i):
+        return pltpu.make_async_copy(buf.at[i], out_ref.at[i], out_sem.at[i])
+
+    @pl.loop(0, count)
+    def _(i):
+        inward(i).start()
+
+    @pl.loop(0, count)
+    def _(i):
+        inward(i).wait()
+        outward(i).start()
+
+    @pl.loop(0, count)
+    def _(i):
+        outward(i).wait()
+
+
+def place_kernel(arrives_ref, lengths_ref, arrived_ref, fresh_ref, out_ref, buf, in_sem, out_sem):
+    count = buf.shape[0]
+    per_unit = MAXCTX // PAGE
+
+    def inward(i):
+        return pltpu.make_async_copy(arrived_ref.at[arrives_ref[i]], buf.at[i], in_sem.at[i])
+
+    def outward(i):
+        return pltpu.make_async_copy(buf.at[i], out_ref.at[i], out_sem.at[i])
+
+    @pl.loop(0, count)
+    def _(i):
+        inward(i).start()
+
+    @pl.loop(0, count)
+    def _(i):
+        inward(i).wait()
+        slot = i // per_unit
+        for step in range(2):
+            position = lengths_ref[slot] + step
+
+            @pl.when(position // PAGE == i % per_unit)
+            def _():
+                row = position % PAGE
+                base = pl.multiple_of((row // 16) * 16, 16)
+                tile = buf[i, pl.ds(base, 16), :]
+                line = lax.broadcasted_iota(jnp.int32, tile.shape, 0)
+                new = jnp.broadcast_to(fresh_ref[slot, step : step + 1, :], tile.shape)
+                mixed = jnp.where(line == row - base, new, tile.astype(jnp.float32))
+                buf[i, pl.ds(base, 16), :] = mixed.astype(jnp.bfloat16)
+
+        outward(i).start()
+
+    @pl.loop(0, count)
+    def _(i):
+        outward(i).wait()
+
+
+NT = (((1,), (1,)), ((), ()))
+
+
+def layer_kernel(
+    devices, capacity,
+    table, hidden_ref, cos_ref, sin_ref, qkv_hbm, out_hbm, pages_hbm,
+    arrived_hbm, mixed_ref, fresh_ref,
+    qkv_w, out_w, pages, rows_all, spread, queries, new_keys, new_values, part_out, part_in, att_all, flat,
+    load_sem, page_send, page_recv, row_send, row_recv, part_send, part_recv, att_send, att_recv,
+    self_sem,
+):
+    me = lax.axis_index("tp")
+    pages_dev = pages.shape[0]
+    rows = hidden_ref.shape[0]
+    requests = rows // 2
+    units = requests * KVH
+    heads = qkv_w.shape[0]
+    tiles = out_w.shape[0]
+    group_count = HEADS // KVH
+    head_rows = group_count + 2
+    score_scale = 1.0 / math.sqrt(HD)
+    span = requests * 2 * group_count
+    at_left, at_arrival, at_slot = pages_dev, 2 * pages_dev, 3 * pages_dev
+    at_own = at_slot + units
+    at_head, at_request = at_own + U_DEV, at_own + 2 * U_DEV
+
+    def peer(offset):
+        return lax.rem(me + offset, devices)
+
+    def sender(offset):
+        return lax.rem(me + devices - offset, devices)
+
+    def remote(src, dst, send, recv, offset):
+        return pltpu.make_async_remote_copy(
+            src_ref=src, dst_ref=dst, send_sem=send, recv_sem=recv,
+            device_id={"tp": peer(offset)}, device_id_type=pl.DeviceIdType.MESH,
+        )
+
+    def page_copy(rank, offset):
+        return remote(
+            pages_hbm.at[peer(offset) * capacity + rank], arrived_hbm.at[me * capacity + rank],
+            page_send.at[rank, offset], page_recv.at[rank, offset], offset,
+        )
+
+    def page_arrival(rank, offset):
+        at = sender(offset) * capacity + rank
+        return remote(
+            pages_hbm.at[at], arrived_hbm.at[at],
+            page_send.at[rank, offset], page_recv.at[rank, offset], offset,
+        )
+
+    def row_copy(offset, owner):
+        return remote(
+            rows_all.at[owner], rows_all.at[owner], row_send.at[offset], row_recv.at[offset], offset
+        )
+
+    def part_copy(offset, src, dst):
+        return remote(
+            part_out.at[src], part_in.at[dst], part_send.at[offset], part_recv.at[offset], offset
+        )
+
+    def att_copy(offset, owner):
+        block = att_all.at[pl.ds(owner * U_DEV, U_DEV)]
+        return remote(block, block, att_send.at[offset], att_recv.at[offset], offset)
+
+    def send_pages(rank):
+        @pl.loop(1, devices)
+        def _(offset):
+            page_copy(rank, offset).start()
+
+    barrier = pltpu.get_barrier_semaphore()
+
+    @pl.loop(1, devices)
+    def _(offset):
+        pl.semaphore_signal(
+            barrier, inc=1, device_id={"tp": peer(offset)}, device_id_type=pl.DeviceIdType.MESH
+        )
+
+    loads = [
+        pltpu.make_async_copy(qkv_hbm.at[pl.ds(c * HD, HD)], qkv_w.at[c], load_sem.at[c])
+        for c in range(heads)
+    ]
+    loads.append(pltpu.make_async_copy(pages_hbm, pages, load_sem.at[heads]))
+    loads += [
+        pltpu.make_async_copy(
+            out_hbm.at[pl.ds(c * HD, HD)], out_w.at[c], load_sem.at[heads + 1 + c]
+        )
+        for c in range(tiles)
+    ]
+    for load in loads[: heads + 1]:
+        load.start()
+    pl.semaphore_wait(barrier, devices - 1)
+    send_pages(0)
+
+    for c in range(heads):
+        loads[c].wait()
+        part = lax.dot_general(
+            hidden_ref[...], qkv_w[c], NT, preferred_element_type=jnp.float32
+        ).astype(jnp.bfloat16).astype(jnp.float32)
+        turned = part * cos_ref[...] + pltpu.roll(part, HD // 2, 1) * sin_ref[...]
+        is_value = lax.rem(me * heads + c, head_rows) == head_rows - 1
+        rows_all[me, c] = jnp.where(is_value, part, turned).astype(jnp.bfloat16)
+
+    @pl.loop(1, devices)
+    def _(offset):
+        row_copy(offset, me).start()
+
+    if capacity > 1:
+        send_pages(1)
+    for load in loads[heads + 1 :]:
+        load.start()
+    loads[heads].wait()
+    own_pages = pltpu.make_async_copy(
+        pages.at[pl.ds(me * capacity, capacity)],
+        arrived_hbm.at[pl.ds(me * capacity, capacity)],
+        self_sem,
+    )
+    own_pages.start()
+
+    @pl.loop(1, devices)
+    def _(offset):
+        row_copy(offset, sender(offset)).wait_recv()
+
+    for h in range(KVH):
+        for g in range(group_count):
+            at = h * head_rows + g
+            spread[pl.ds(h * span + g, rows, stride=group_count), :] = rows_all[
+                at // heads, at % heads
+            ].astype(jnp.float32)
+        at = h * head_rows + group_count
+        new_keys[h] = rows_all[at // heads, at % heads]
+        new_values[h] = rows_all[(at + 1) // heads, (at + 1) % heads]
+        for r in range(requests):
+            start = h * span + r * 2 * group_count
+            queries[h * requests + r] = spread[start : start + 2 * group_count, :].astype(
+                jnp.bfloat16
+            )
+
+    lane = lax.broadcasted_iota(jnp.int32, (2 * group_count, PAGE), 1)
+    strip = PAGE // capacity
+
+    @pl.loop(0, devices)
+    def _(target):
+        sums = jnp.zeros((2 * group_count, PAGE), jnp.float32)
+        for rank in range(capacity):
+            query = queries[table[target * capacity + rank]]
+            left = table[at_left + target * capacity + rank]
+            page = pages[target * capacity + rank]
+            scores = lax.dot_general(
+                query, page[:, :HD], NT, preferred_element_type=jnp.float32
+            ) * score_scale
+            weights = jnp.where(lane < left, jnp.exp(scores), 0.0)
+            total = jnp.sum(weights, axis=-1, keepdims=True)
+            weighted = jnp.dot(
+                weights.astype(jnp.bfloat16), page[:, HD:], preferred_element_type=jnp.float32
+            )
+            part_out[target, rank] = weighted.astype(jnp.bfloat16)
+            high = total.astype(jnp.bfloat16).astype(jnp.float32)
+            sums = jnp.where(lane == rank * strip, high, sums)
+            sums = jnp.where(lane == rank * strip + strip // 2, total - high, sums)
+        part_out[target, capacity] = sums.astype(jnp.bfloat16)
+
+    @pl.loop(1, devices)
+    def _(offset):
+        part_copy(offset, peer(offset), me).start()
+
+    if capacity > 2:
+        send_pages(2)
+    part_in[me] = part_out[me]
+
+    own_sums, own_totals = [], []
+    row = lax.broadcasted_iota(jnp.int32, (2 * group_count, rows), 0)
+    col = lax.broadcasted_iota(jnp.int32, (2 * group_count, rows), 1)
+    line = lax.broadcasted_iota(jnp.int32, (rows, HD), 0)
+    for j in range(U_DEV):
+        request = table[at_request + j]
+        keys = new_keys[table[at_head + j]]
+        values = new_values[table[at_head + j]]
+        scores = lax.dot_general(
+            queries[table[at_own + j]], keys, NT, preferred_element_type=jnp.float32
+        ) * score_scale
+        seen = (col // 2 == request) & (col % 2 <= row // group_count)
+        weights = jnp.where(seen, jnp.exp(scores), 0.0)
+        own_totals.append(jnp.sum(weights, axis=-1, keepdims=True))
+        own_sums.append(
+            jnp.dot(weights.astype(jnp.bfloat16), values, preferred_element_type=jnp.float32)
+        )
+        for step in range(2):
+            mine = line == request * 2 + step
+            for half, kind in ((0, keys), (1, values)):
+                fresh_ref[j, step : step + 1, half * HD : (half + 1) * HD] = jnp.sum(
+                    jnp.where(mine, kind.astype(jnp.float32), 0.0), axis=0, keepdims=True
+                )
+
+    @pl.loop(1, devices)
+    def _(offset):
+        part_copy(offset, me, sender(offset)).wait_recv()
+
+    def gather_parts(source, carry):
+        sums, totals = carry
+        tails = part_in[source, capacity].astype(jnp.float32)
+        for rank in range(capacity):
+            slot = table[at_arrival + source * capacity + rank]
+            part = part_in[source, rank].astype(jnp.float32)
+            total = jnp.sum(
+                jnp.where(lane // strip == rank, tails, 0.0), axis=-1, keepdims=True
+            )
+            sums = tuple(s + jnp.where(slot == j, part, 0.0) for j, s in enumerate(sums))
+            totals = tuple(t + jnp.where(slot == j, total, 0.0) for j, t in enumerate(totals))
+        return sums, totals
+
+    sums, totals = lax.fori_loop(0, devices, gather_parts, (tuple(own_sums), tuple(own_totals)))
+    for j in range(U_DEV):
+        att_all[me * U_DEV + j] = (sums[j] / totals[j]).astype(jnp.bfloat16)
+
+    @pl.loop(1, devices)
+    def _(offset):
+        att_copy(offset, me).start()
+
+    for rank in range(3, capacity):
+        send_pages(rank)
+
+    @pl.loop(1, devices)
+    def _(offset):
+        att_copy(offset, sender(offset)).wait_recv()
+
+    for r in range(requests):
+        for h in range(KVH):
+            slot = table[at_slot + r * KVH + h]
+            spread[h * span + r * 2 * group_count : h * span + (r + 1) * 2 * group_count, :] = (
+                att_all[slot].astype(jnp.float32)
+            )
+    for h in range(KVH):
+        for g in range(group_count):
+            at = (h * group_count + g) * HD
+            flat[:, at : at + HD] = spread[
+                pl.ds(h * span + g, rows, stride=group_count), :
+            ].astype(jnp.bfloat16)
+    for c in range(tiles):
+        loads[heads + 1 + c].wait()
+        mixed_ref[:, c * HD : (c + 1) * HD] = lax.dot_general(
+            flat[...], out_w[c], NT, preferred_element_type=jnp.float32
+        ).astype(jnp.bfloat16)
+
+    own_pages.wait()
+
+    @pl.loop(1, devices)
+    def _(offset):
+        row_copy(offset, me).wait_send()
+        part_copy(offset, peer(offset), me).wait_send()
+        att_copy(offset, me).wait_send()
+        for rank in range(capacity):
+            page_copy(rank, offset).wait_send()
+            page_arrival(rank, offset).wait_recv()
+
+
+def fused_body(hidden_states, qkv_weight, out_weight, cache_pages, context_lengths, new_units, old_pages):
+    devices = lax.axis_size("tp")
+    requests = hidden_states.shape[0]
+    rows = requests * 2
+    pages_dev = cache_pages.shape[0]
+    capacity = pages_dev // devices
+    heads = qkv_weight.shape[0] // HD
+    tiles = out_weight.shape[0] // HD
+    group_count = HEADS // KVH
+    units = new_units.shape[0]
+    hbm = pl.BlockSpec(memory_space=pl.ANY)
+    vmem = pl.BlockSpec(memory_space=pltpu.VMEM)
+    smem = pl.BlockSpec(memory_space=pltpu.SMEM)
+    dma = pltpu.SemaphoreType.DMA
+    send_order, arrives_at, table = index_tables(
+        context_lengths, new_units, old_pages, pages_dev
+    )
+    positions = (
+        context_lengths[:, None] + jnp.arange(2, dtype=jnp.int32)[None, :]
+    ).reshape(rows).astype(jnp.float32)
+    half = HD // 2
+    frequency = rope_base ** (-(jnp.arange(half, dtype=jnp.float32) * 2.0 / HD))
+    angles = positions[:, None] * frequency
+    cosine, sine = jnp.cos(angles), jnp.sin(angles)
+    cosine = jnp.concatenate([cosine, cosine], axis=-1)
+    sine = jnp.concatenate([-sine, sine], axis=-1)
+
+    buffers = [
+        pltpu.VMEM(cache_pages.shape, jnp.bfloat16), dma((pages_dev,)), dma((pages_dev,)),
+    ]
+    outgoing = pl.pallas_call(
+        sort_kernel,
+        out_shape=jax.ShapeDtypeStruct(cache_pages.shape, jnp.bfloat16),
+        in_specs=[smem, hbm],
+        out_specs=hbm,
+        scratch_shapes=buffers,
+        name="sort_pages",
+    )(send_order, cache_pages)
+    tile = (2 * group_count, HD)
+    arrived, mixed, fresh = pl.pallas_call(
+        lambda *refs: layer_kernel(devices, capacity, *refs),
+        out_shape=(
+            jax.ShapeDtypeStruct(cache_pages.shape, jnp.bfloat16),
+            jax.ShapeDtypeStruct((rows, out_weight.shape[0]), jnp.bfloat16),
+            jax.ShapeDtypeStruct((U_DEV, 2, 2 * HD), jnp.float32),
+        ),
+        in_specs=[smem, vmem, vmem, vmem, hbm, hbm, hbm],
+        out_specs=(hbm, vmem, vmem),
+        scratch_shapes=[
+            pltpu.VMEM((heads, HD, D), jnp.bfloat16),
+            pltpu.VMEM((tiles, HD, HEADS * HD), jnp.bfloat16),
+            pltpu.VMEM(cache_pages.shape, jnp.bfloat16),
+            pltpu.VMEM((devices, heads, rows, HD), jnp.bfloat16),
+            pltpu.VMEM((units * 2 * group_count, HD), jnp.float32),
+            pltpu.VMEM((units,) + tile, jnp.bfloat16),
+            pltpu.VMEM((KVH, rows, HD), jnp.bfloat16),
+            pltpu.VMEM((KVH, rows, HD), jnp.bfloat16),
+            pltpu.VMEM((devices, capacity + 1) + tile, jnp.bfloat16),
+            pltpu.VMEM((devices, capacity + 1) + tile, jnp.bfloat16),
+            pltpu.VMEM((units,) + tile, jnp.bfloat16),
+            pltpu.VMEM((rows, HEADS * HD), jnp.bfloat16),
+            dma((heads + 1 + tiles,)),
+            dma((capacity, devices)), dma((capacity, devices)),
+            dma((devices,)), dma((devices,)),
+            dma((devices,)), dma((devices,)),
+            dma((devices,)), dma((devices,)),
+            dma(()),
+        ],
+        compiler_params=pltpu.CompilerParams(
+            collective_id=0, has_side_effects=True, vmem_limit_bytes=48 << 20
+        ),
+        name="layer",
+    )(table, hidden_states.reshape(rows, D), cosine, sine, qkv_weight, out_weight, outgoing)
+    own_lengths = jnp.take(
+        context_lengths,
+        lax.dynamic_slice_in_dim(new_units, lax.axis_index("tp") * U_DEV, U_DEV) // KVH,
+    )
+    placed = pl.pallas_call(
+        place_kernel,
+        out_shape=jax.ShapeDtypeStruct(cache_pages.shape, jnp.bfloat16),
+        in_specs=[smem, smem, hbm, vmem],
+        out_specs=hbm,
+        scratch_shapes=buffers,
+        name="place_pages",
+    )(arrives_at, own_lengths, arrived, fresh)
+    return (mixed.reshape(requests, 2, out_weight.shape[0]), placed)
+
+
+def body(hidden_states, qkv_weight, out_weight, cache_pages, context_lengths, new_units, old_pages):
+    devices = lax.axis_size("tp")
+    whole_heads = qkv_weight.shape[0] % HD == 0 and out_weight.shape[0] % HD == 0
+    whole_shares = cache_pages.shape[0] % devices == 0 and hidden_states.shape[0] == KVH
+    chosen = fused_body if whole_heads and whole_shares else plain_body
+    return chosen(
+        hidden_states, qkv_weight, out_weight, cache_pages, context_lengths, new_units, old_pages
+    )
+
+
 def solution(mesh):
     in_specs = (
         P("group", None, None),

time: 181 us -> 145 us (0.80)
  the two profiles are of different devices: /device:TPU:1 before, /device:TPU:31 now
where the time goes in v1:
time: 145 us
  Pallas kernels  132 us (91%)
  other arithmetic  6.71 us (5%)
  local copies, waits for them, and re-layouts  5.72 us (4%)
    pallas_call x1, Pallas kernels, fused_body(): pl.pallas_call(lambda *refs: layer_kernel(devices, capacity, *refs), out_...  120 us
    pallas_call x1, Pallas kernels, fused_body(): pl.pallas_call(place_kernel, out_shape=jax.ShapeDtypeStruct(cache_pages.s...  6.18 us
    pallas_call x1, Pallas kernels, fused_body(): pl.pallas_call(sort_kernel, out_shape=jax.ShapeDtypeStruct(cache_pages.sh...  5.83 us
    reduce_sum x5, other arithmetic, pick(): return jnp.sum(jnp.where(hit, values[None, :], 0), axis=1)  3.19 us

profile of v1, /device:TPU:31, one launch (start us, length us, event | category | flops | bytes accessed | tf_op | source)
XLA Modules:
  0.0 145.0 jit_solution(10095172073932285200)
XLA Ops:
  0.6 0.8 and_select_fusion.10
  1.4 0.8 select_reduce_fusion.2
  2.3 0.2 convert_reduce_fusion.1
  2.5 0.6 select_reduce_fusion.1
  3.1 0.7 select_reduce_fusion.6
  3.9 0.7 compare_select_fusion
  4.6 0.1 iota_add_fusion
  4.7 0.1 add.132
  4.8 0.9 select_reduce_fusion
  5.7 0.2 convert_reduce_fusion
  5.9 0.0 copy-start.2
  5.9 0.1 select_reduce_fusion.3
  6.0 1.3 gather_fusion
  7.3 0.5 multiply_add_fusion
  7.9 0.1 concatenate.9.refs_0_
  7.9 0.7 add_convert_fusion
  8.7 0.1 convert_element_type.19
  8.8 0.1 fusion.1
  8.9 0.1 pad_maximum_fusion
  9.0 1.1 reshape.185.refs_1_
  10.0 5.8 %sort_pages.1.refs_6_ = bf16[64,128,256]{2,1,0:T(8,128)(2,1)} custom-call(s32[64]{0:T(128)} %get-tuple-element.8.order_ref, bf16[64,128,256]{2,1,0:T(8,128)(2,1)} %pages_ref.1), custom_call_target="tpu_custom_call" | custom-call | tf_op jit(solution)/shard_map/sort_pages/pallas_call | solution.py:584
  15.9 0.0 copy-done.2
  15.9 119.8 %layer.1 = (bf16[64,128,256]{2,1,0:T(8,128)(2,1)S(1)}, bf16[16,512]{1,0:T(8,128)(2,1)S(1)}, f32[4,2,256]{2,1,0:T(2,128)S(1)}) custom-call(s32[268]{0:T(512)S(1)} %concatenate.9.refs_0_, bf16[16,8192]{1,0:T(8,128)(2,1)S(1)} %reshape.185.refs_1_, f32[16,128]{1,0:T(8,128)S(1)} %get-tuple-element.28.refs_2_, f32[16,128]{1,0:T(8,128)S(1)} %get-tuple-element.29.refs_3_, ...), custom_call_target="tpu_custom_call" | custom-call | tf_op jit(solution)/shard_map/layer/pallas_call | solution.py:593
  135.7 0.0 copy-start
  135.7 1.9 %copy-done = bf16[64,128,256]{2,1,0:T(8,128)(2,1)} copy-done((bf16[64,128,256]{2,1,0:T(8,128)(2,1)}, bf16[64,128,256]{2,1,0:T(8,128)(2,1)S(1)}, u32[]{:S(2)}) %copy-start) | copy-done | bytes 4194328
  137.6 0.0 copy-start.1
  137.6 0.6 copy-done.1
  138.2 0.6 reshape.186
  138.8 6.2 %place_pages.1 = bf16[64,128,256]{2,1,0:T(8,128)(2,1)} custom-call(s32[64]{0:T(128)} %copy-done.2, s32[4]{0:T(128)} %get-tuple-element.24.lengths_ref, bf16[64,128,256]{2,1,0:T(8,128)(2,1)} %copy-done, f32[4,2,256]{2,1,0:T(2,128)} %copy-done.1), custom_call_target="tpu_custom_call" | custom-call | tf_op jit(solution)/shard_map/place_pages/pallas_call | solution.py:631
  (8 shorter events, 0.1 us)
Async XLA Ops:
  5.9 10.0 %copy-start.2 = (s32[64]{0:T(128)}, s32[64]{0:T(128)S(1)}, u32[]{:S(2)}) copy-start(s32[64]{0:T(128)S(1)} %get-tuple-element.27.arrives_ref) | copy-start | bytes 772
  135.7 1.9 %copy-start = (bf16[64,128,256]{2,1,0:T(8,128)(2,1)}, bf16[64,128,256]{2,1,0:T(8,128)(2,1)S(1)}, u32[]{:S(2)}) copy-start(bf16[64,128,256]{2,1,0:T(8,128)(2,1)S(1)} %get-tuple-element.6.arrived_ref) | copy-start | bytes 12582916
  137.6 0.6 copy-start.1

commit v2 on v1

--- a/solution.py
+++ b/solution.py
@@ -205,6 +205,7 @@
     sent = places[:, None] == sent_at[None, :]
     send_order = pick(sent, places)
     send_ids = pick(sent, local_ids)
+    send_slot = pick(sent, target_slot % U_DEV)
     own_units = lax.dynamic_slice_in_dim(new_units, device * U_DEV, U_DEV)
     wanted = (
         own_units[:, None] * per_unit + jnp.arange(per_unit, dtype=jnp.int32)[None, :]
@@ -214,7 +215,6 @@
     )
     source_dev = source_pos // pages_dev
     arrives_at = source_dev * capacity + ranks(source_dev, source_pos)
-    arrival_slot = pick(places[:, None] == arrives_at[None, :], places // per_unit)
     slot_of_unit = pick(slots[:, None] == new_units[None, :], slots)
     requests = context_lengths.shape[0]
     send_units = send_ids // per_unit
@@ -227,7 +227,7 @@
     own_heads, own_requests = own_units % KVH, own_units // KVH
     table = jnp.concatenate(
         [
-            send_query, send_left, arrival_slot, slot_of_unit,
+            send_query, send_left, send_slot, slot_of_unit,
             own_heads * requests + own_requests, own_heads, own_requests,
         ]
     )
@@ -302,7 +302,7 @@
     devices, capacity,
     table, hidden_ref, cos_ref, sin_ref, qkv_hbm, out_hbm, pages_hbm,
     arrived_hbm, mixed_ref, fresh_ref,
-    qkv_w, out_w, pages, rows_all, spread, queries, new_keys, new_values, part_out, part_in, att_all, flat,
+    qkv_w, out_w, pages, rows_all, spread, queries, new_keys, new_values, part_out, part_in, swap_out, swap_in, att_all, flat,
     load_sem, page_send, page_recv, row_send, row_recv, part_send, part_recv, att_send, att_recv,
     self_sem,
 ):
@@ -317,60 +317,98 @@
     head_rows = group_count + 2
     score_scale = 1.0 / math.sqrt(HD)
     span = requests * 2 * group_count
-    at_left, at_arrival, at_slot = pages_dev, 2 * pages_dev, 3 * pages_dev
+    at_left, at_target, at_slot = pages_dev, 2 * pages_dev, 3 * pages_dev
     at_own = at_slot + units
     at_head, at_request = at_own + U_DEV, at_own + 2 * U_DEV
 
-    def peer(offset):
-        return lax.rem(me + offset, devices)
-
-    def sender(offset):
-        return lax.rem(me + devices - offset, devices)
-
-    def remote(src, dst, send, recv, offset):
+    half = devices // 2
+    here, side = lax.rem(me, half), me // half
+    partner = lax.rem(me + half, devices)
+
+    def near(offset):
+        return side * half + lax.rem(here + offset, half)
+
+    def near_sender(offset):
+        return side * half + lax.rem(here + half - offset, half)
+
+    def far(offset):
+        return (1 - side) * half + lax.rem(here + offset, half)
+
+    def far_sender(offset):
+        return (1 - side) * half + lax.rem(here + half - offset, half)
+
+    def remote(src, dst, send, recv, device):
         return pltpu.make_async_remote_copy(
             src_ref=src, dst_ref=dst, send_sem=send, recv_sem=recv,
-            device_id={"tp": peer(offset)}, device_id_type=pl.DeviceIdType.MESH,
+            device_id={"tp": device}, device_id_type=pl.DeviceIdType.MESH,
         )
 
-    def page_copy(rank, offset):
+    def page_copy(rank, place, device):
         return remote(
-            pages_hbm.at[peer(offset) * capacity + rank], arrived_hbm.at[me * capacity + rank],
-            page_send.at[rank, offset], page_recv.at[rank, offset], offset,
+            pages_hbm.at[device * capacity + rank], arrived_hbm.at[me * capacity + rank],
+            page_send.at[rank, place], page_recv.at[rank, place], device,
         )
 
-    def page_arrival(rank, offset):
-        at = sender(offset) * capacity + rank
+    def page_arrival(rank, place, device):
+        at = device * capacity + rank
         return remote(
             pages_hbm.at[at], arrived_hbm.at[at],
-            page_send.at[rank, offset], page_recv.at[rank, offset], offset,
+            page_send.at[rank, place], page_recv.at[rank, place], device,
         )
 
-    def row_copy(offset, owner):
+    def row_copy(stage, place, owner, device):
+        block = rows_all.at[owner]
+        return remote(block, block, row_send.at[stage, place], row_recv.at[stage, place], device)
+
+    def att_copy(stage, place, owner, device):
+        block = att_all.at[pl.ds(owner * U_DEV, U_DEV)]
+        return remote(block, block, att_send.at[stage, place], att_recv.at[stage, place], device)
+
+    def part_copy(place, src, dst, device):
         return remote(
-            rows_all.at[owner], rows_all.at[owner], row_send.at[offset], row_recv.at[offset], offset
+            part_out.at[src], part_in.at[dst], part_send.at[place], part_recv.at[place], device
         )
 
-    def part_copy(offset, src, dst):
-        return remote(
-            part_out.at[src], part_in.at[dst], part_send.at[offset], part_recv.at[offset], offset
-        )
-
-    def att_copy(offset, owner):
-        block = att_all.at[pl.ds(owner * U_DEV, U_DEV)]
-        return remote(block, block, att_send.at[offset], att_recv.at[offset], offset)
-
-    def send_pages(rank):
-        @pl.loop(1, devices)
+    def swap_copy():
+        return remote(swap_out, swap_in, part_send.at[0], part_recv.at[0], partner)
+
+    batches = 2 * capacity
+
+    def send_pages(batch):
+        if batch >= batches:
+            return
+        rank, low, high = batch // 2, (batch % 2) * (half // 2), (batch % 2 + 1) * (half // 2)
+        if batch % 2:
+            high = half
+
+        if low == 0:
+            page_copy(rank, 0, partner).start()
+
+        @pl.loop(max(low, 1), high)
         def _(offset):
-            page_copy(rank, offset).start()
+            page_copy(rank, offset, far(offset)).start()
+            page_copy(rank, half + offset, near(offset)).start()
+
+    def pack_totals(values):
+        packed = jnp.zeros((2 * group_count, PAGE), jnp.float32)
+        for j, total in enumerate(values):
+            top = total.astype(jnp.bfloat16).astype(jnp.float32)
+            packed = jnp.where(lane == j * strip, top, packed)
+            packed = jnp.where(lane == j * strip + strip // 2, total - top, packed)
+        return packed.astype(jnp.bfloat16)
+
+    def unpack_total(packed, j):
+        return jnp.sum(jnp.where(lane // strip == j, packed, 0.0), axis=-1, keepdims=True)
+
+    lane = lax.broadcasted_iota(jnp.int32, (2 * group_count, PAGE), 1)
+    strip = PAGE // U_DEV
 
     barrier = pltpu.get_barrier_semaphore()
 
     @pl.loop(1, devices)
     def _(offset):
         pl.semaphore_signal(
-            barrier, inc=1, device_id={"tp": peer(offset)}, device_id_type=pl.DeviceIdType.MESH
+            barrier, inc=1, device_id={"tp": lax.rem(me + offset, devices)}, device_id_type=pl.DeviceIdType.MESH
         )
 
     loads = [
@@ -398,12 +436,13 @@
         is_value = lax.rem(me * heads + c, head_rows) == head_rows - 1
         rows_all[me, c] = jnp.where(is_value, part, turned).astype(jnp.bfloat16)
 
-    @pl.loop(1, devices)
-    def _(offset):
-        row_copy(offset, me).start()
-
-    if capacity > 1:
-        send_pages(1)
+    row_copy(0, 0, me, partner).start()
+
+    @pl.loop(1, half)
+    def _(offset):
+        row_copy(0, offset, me, near(offset)).start()
+
+    send_pages(1)
     for load in loads[heads + 1 :]:
         load.start()
     loads[heads].wait()
@@ -414,9 +453,19 @@
     )
     own_pages.start()
 
-    @pl.loop(1, devices)
-    def _(offset):
-        row_copy(offset, sender(offset)).wait_recv()
+    row_copy(0, 0, partner, partner).wait_recv()
+
+    @pl.loop(1, half)
+    def _(offset):
+        row_copy(1, offset, partner, near(offset)).start()
+
+    send_pages(2)
+
+    @pl.loop(1, half)
+    def _(offset):
+        source = near_sender(offset)
+        row_copy(0, offset, source, source).wait_recv()
+        row_copy(1, offset, lax.rem(source + half, devices), source).wait_recv()
 
     for h in range(KVH):
         for g in range(group_count):
@@ -433,12 +482,10 @@
                 jnp.bfloat16
             )
 
-    lane = lax.broadcasted_iota(jnp.int32, (2 * group_count, PAGE), 1)
-    strip = PAGE // capacity
-
     @pl.loop(0, devices)
     def _(target):
-        sums = jnp.zeros((2 * group_count, PAGE), jnp.float32)
+        zero = jnp.zeros((2 * group_count, PAGE), jnp.float32)
+        sums, totals = [zero] * U_DEV, [zero[:, :1]] * U_DEV
         for rank in range(capacity):
             query = queries[table[target * capacity + rank]]
             left = table[at_left + target * capacity + rank]
@@ -451,19 +498,20 @@
             weighted = jnp.dot(
                 weights.astype(jnp.bfloat16), page[:, HD:], preferred_element_type=jnp.float32
             )
-            part_out[target, rank] = weighted.astype(jnp.bfloat16)
-            high = total.astype(jnp.bfloat16).astype(jnp.float32)
-            sums = jnp.where(lane == rank * strip, high, sums)
-            sums = jnp.where(lane == rank * strip + strip // 2, total - high, sums)
-        part_out[target, capacity] = sums.astype(jnp.bfloat16)
-
-    @pl.loop(1, devices)
-    def _(offset):
-        part_copy(offset, peer(offset), me).start()
-
-    if capacity > 2:
-        send_pages(2)
-    part_in[me] = part_out[me]
+            slot = table[at_target + target * capacity + rank]
+            for j in range(U_DEV):
+                sums[j] = sums[j] + jnp.where(slot == j, weighted, 0.0)
+                totals[j] = totals[j] + jnp.where(slot == j, total, 0.0)
+        place, which = lax.rem(target, half), target // half
+        for j in range(U_DEV):
+            part_out[place, which, j] = sums[j].astype(jnp.bfloat16)
+        part_out[place, which, U_DEV] = pack_totals(totals)
+
+    @pl.loop(1, half)
+    def _(offset):
+        part_copy(offset, lax.rem(here + offset, half), here, near(offset)).start()
+
+    send_pages(3)
 
     own_sums, own_totals = [], []
     row = lax.broadcasted_iota(jnp.int32, (2 * group_count, rows), 0)
@@ -484,42 +532,61 @@
         )
         for step in range(2):
             mine = line == request * 2 + step
-            for half, kind in ((0, keys), (1, values)):
-                fresh_ref[j, step : step + 1, half * HD : (half + 1) * HD] = jnp.sum(
+            for part, kind in ((0, keys), (1, values)):
+                fresh_ref[j, step : step + 1, part * HD : (part + 1) * HD] = jnp.sum(
                     jnp.where(mine, kind.astype(jnp.float32), 0.0), axis=0, keepdims=True
                 )
 
-    @pl.loop(1, devices)
-    def _(offset):
-        part_copy(offset, me, sender(offset)).wait_recv()
-
-    def gather_parts(source, carry):
-        sums, totals = carry
-        tails = part_in[source, capacity].astype(jnp.float32)
-        for rank in range(capacity):
-            slot = table[at_arrival + source * capacity + rank]
-            part = part_in[source, rank].astype(jnp.float32)
-            total = jnp.sum(
-                jnp.where(lane // strip == rank, tails, 0.0), axis=-1, keepdims=True
-            )
-            sums = tuple(s + jnp.where(slot == j, part, 0.0) for j, s in enumerate(sums))
-            totals = tuple(t + jnp.where(slot == j, total, 0.0) for j, t in enumerate(totals))
-        return sums, totals
-
-    sums, totals = lax.fori_loop(0, devices, gather_parts, (tuple(own_sums), tuple(own_totals)))
+    @pl.loop(1, half)
+    def _(offset):
+        source = near_sender(offset)
+        part_copy(offset, here, lax.rem(here + half - offset, half), source).wait_recv()
+
+    def half_sum(which):
+        def add(offset, carry):
+            block = part_in.at[lax.rem(here + offset, half), which]
+            return tuple(c + block[j].astype(jnp.float32) for j, c in enumerate(carry))
+
+        first = tuple(
+            part_out[here, which, j].astype(jnp.float32) for j in range(U_DEV + 1)
+        )
+        return lax.fori_loop(1, half, add, first)
+
+    away = half_sum(1 - side)
     for j in range(U_DEV):
-        att_all[me * U_DEV + j] = (sums[j] / totals[j]).astype(jnp.bfloat16)
-
-    @pl.loop(1, devices)
-    def _(offset):
-        att_copy(offset, me).start()
-
-    for rank in range(3, capacity):
-        send_pages(rank)
-
-    @pl.loop(1, devices)
-    def _(offset):
-        att_copy(offset, sender(offset)).wait_recv()
+        swap_out[j] = away[j].astype(jnp.bfloat16)
+    swap_out[U_DEV] = pack_totals([unpack_total(away[U_DEV], j) for j in range(U_DEV)])
+    kept = half_sum(side)
+    swap_copy().start()
+    send_pages(4)
+    swap_copy().wait_recv()
+    packed = kept[U_DEV] + swap_in[U_DEV].astype(jnp.float32)
+    for j in range(U_DEV):
+        total = own_totals[j] + unpack_total(packed, j)
+        weighted = own_sums[j] + kept[j] + swap_in[j].astype(jnp.float32)
+        att_all[me * U_DEV + j] = (weighted / total).astype(jnp.bfloat16)
+
+    att_copy(0, 0, me, partner).start()
+
+    @pl.loop(1, half)
+    def _(offset):
+        att_copy(0, offset, me, near(offset)).start()
+
+    send_pages(5)
+    att_copy(0, 0, partner, partner).wait_recv()
+
+    @pl.loop(1, half)
+    def _(offset):
+        att_copy(1, offset, partner, near(offset)).start()
+
+    for batch in range(6, batches):
+        send_pages(batch)
+
+    @pl.loop(1, half)
+    def _(offset):
+        source = near_sender(offset)
+        att_copy(0, offset, source, source).wait_recv()
+        att_copy(1, offset, lax.rem(source + half, devices), source).wait_recv()
 
     for r in range(requests):
         for h in range(KVH):
@@ -541,14 +608,27 @@
 
     own_pages.wait()
 
-    @pl.loop(1, devices)
-    def _(offset):
-        row_copy(offset, me).wait_send()
-        part_copy(offset, peer(offset), me).wait_send()
-        att_copy(offset, me).wait_send()
-        for rank in range(capacity):
-            page_copy(rank, offset).wait_send()
-            page_arrival(rank, offset).wait_recv()
+    row_copy(0, 0, me, partner).wait_send()
+    att_copy(0, 0, me, partner).wait_send()
+    swap_copy().wait_send()
+
+    @pl.loop(1, half)
+    def _(offset):
+        for stage, owner in ((0, me), (1, partner)):
+            row_copy(stage, offset, owner, near(offset)).wait_send()
+            att_copy(stage, offset, owner, near(offset)).wait_send()
+        part_copy(offset, lax.rem(here + offset, half), here, near(offset)).wait_send()
+
+    for rank in range(capacity):
+        page_copy(rank, 0, partner).wait_send()
+        page_arrival(rank, 0, partner).wait_recv()
+
+        @pl.loop(1, half)
+        def _(offset):
+            page_copy(rank, offset, far(offset)).wait_send()
+            page_arrival(rank, offset, far_sender(offset)).wait_recv()
+            page_copy(rank, half + offset, near(offset)).wait_send()
+            page_arrival(rank, half + offset, near_sender(offset)).wait_recv()
 
 
 def fused_body(hidden_states, qkv_weight, out_weight, cache_pages, context_lengths, new_units, old_pages):
@@ -608,15 +688,17 @@
             pltpu.VMEM((units,) + tile, jnp.bfloat16),
             pltpu.VMEM((KVH, rows, HD), jnp.bfloat16),
             pltpu.VMEM((KVH, rows, HD), jnp.bfloat16),
-            pltpu.VMEM((devices, capacity + 1) + tile, jnp.bfloat16),
-            pltpu.VMEM((devices, capacity + 1) + tile, jnp.bfloat16),
+            pltpu.VMEM((devices // 2, 2, U_DEV + 1) + tile, jnp.bfloat16),
+            pltpu.VMEM((devices // 2, 2, U_DEV + 1) + tile, jnp.bfloat16),
+            pltpu.VMEM((U_DEV + 1,) + tile, jnp.bfloat16),
+            pltpu.VMEM((U_DEV + 1,) + tile, jnp.bfloat16),
             pltpu.VMEM((units,) + tile, jnp.bfloat16),
             pltpu.VMEM((rows, HEADS * HD), jnp.bfloat16),
             dma((heads + 1 + tiles,)),
             dma((capacity, devices)), dma((capacity, devices)),
-            dma((devices,)), dma((devices,)),
-            dma((devices,)), dma((devices,)),
-            dma((devices,)), dma((devices,)),
+            dma((2, devices // 2)), dma((2, devices // 2)),
+            dma((devices // 2,)), dma((devices // 2,)),
+            dma((2, devices // 2)), dma((2, devices // 2)),
             dma(()),
         ],
         compiler_params=pltpu.CompilerParams(
@@ -642,7 +724,7 @@
 def body(hidden_states, qkv_weight, out_weight, cache_pages, context_lengths, new_units, old_pages):
     devices = lax.axis_size("tp")
     whole_heads = qkv_weight.shape[0] % HD == 0 and out_weight.shape[0] % HD == 0
-    whole_shares = cache_pages.shape[0] % devices == 0 and hidden_states.shape[0] == KVH
+    whole_shares = cache_pages.shape[0] % devices == 0 and devices % 4 == 0 and hidden_states.shape[0] == KVH
     chosen = fused_body if whole_heads and whole_shares else plain_body
     return chosen(
         hidden_states, qkv_weight, out_weight, cache_pages, context_lengths, new_units, old_pages

time: 145 us -> 132 us (0.910)
  the two profiles are of different devices: /device:TPU:31 before, /device:TPU:1 now
where the time goes in v2:
time: 132 us
  Pallas kernels  118 us (89%)
  other arithmetic  7.19 us (5%)
  local copies, waits for them, and re-layouts  5.72 us (4%)
    pallas_call x1, Pallas kernels, fused_body(): pl.pallas_call(lambda *refs: layer_kernel(devices, capacity, *refs), out_...  106 us
    pallas_call x1, Pallas kernels, fused_body(): pl.pallas_call(place_kernel, out_shape=jax.ShapeDtypeStruct(cache_pages.s...  6.11 us
    pallas_call x1, Pallas kernels, fused_body(): pl.pallas_call(sort_kernel, out_shape=jax.ShapeDtypeStruct(cache_pages.sh...  5.83 us
    reduce_sum x4, other arithmetic, pick(): return jnp.sum(jnp.where(hit, values[None, :], 0), axis=1)  3.09 us

profile of v2, /device:TPU:1, one launch (start us, length us, event | category | flops | bytes accessed | tf_op | source)
XLA Modules:
  0.0 132.0 jit_solution(7510570502371101558)
XLA Ops:
  0.6 0.8 and_select_fusion.10
  1.4 0.8 select_reduce_fusion.2
  2.3 0.2 convert_reduce_fusion.1
  2.5 0.6 select_reduce_fusion.1
  3.1 0.7 select_reduce_fusion.6
  3.9 0.7 compare_select_fusion
  4.6 0.1 iota_add_fusion
  4.7 0.1 add.138
  4.8 0.9 select_reduce_fusion
  5.7 0.2 convert_reduce_fusion
  5.9 0.6 multiply_add_fusion.arrives_ref
  6.5 1.3 gather_fusion
  7.8 0.5 multiply_add_fusion.1
  8.3 0.1 concatenate.9.refs_0_
  8.4 0.7 add_convert_fusion
  9.1 0.1 convert_element_type.18
  9.2 0.1 fusion.1
  9.3 0.1 pad_maximum_fusion
  9.4 1.1 reshape.179.refs_1_
  10.5 5.8 %sort_pages.1.refs_6_ = bf16[64,128,256]{2,1,0:T(8,128)(2,1)} custom-call(s32[64]{0:T(128)} %get-tuple-element.8.order_ref, bf16[64,128,256]{2,1,0:T(8,128)(2,1)} %pages_ref.1), custom_call_target="tpu_custom_call" | custom-call | tf_op jit(solution)/shard_map/sort_pages/pallas_call | solution.py:664
  16.3 106.4 %layer.1 = (bf16[64,128,256]{2,1,0:T(8,128)(2,1)S(1)}, bf16[16,512]{1,0:T(8,128)(2,1)S(1)}, f32[4,2,256]{2,1,0:T(2,128)S(1)}) custom-call(s32[268]{0:T(512)S(1)} %concatenate.9.refs_0_, bf16[16,8192]{1,0:T(8,128)(2,1)S(1)} %reshape.179.refs_1_, f32[16,128]{1,0:T(8,128)S(1)} %get-tuple-element.29.refs_2_, f32[16,128]{1,0:T(8,128)S(1)} %get-tuple-element.30.refs_3_, ...), custom_call_target="tpu_custom_call" | custom-call | tf_op jit(solution)/shard_map/layer/pallas_call | solution.py:673
  122.7 0.0 copy-start
  122.7 1.9 %copy-done = bf16[64,128,256]{2,1,0:T(8,128)(2,1)} copy-done((bf16[64,128,256]{2,1,0:T(8,128)(2,1)}, bf16[64,128,256]{2,1,0:T(8,128)(2,1)S(1)}, u32[]{:S(2)}) %copy-start) | copy-done | bytes 4194328
  124.7 0.0 copy-start.1
  124.7 0.6 copy-done.1
  125.3 0.6 reshape.180
  125.9 6.1 %place_pages.1 = bf16[64,128,256]{2,1,0:T(8,128)(2,1)} custom-call(s32[64]{0:T(128)} %multiply_add_fusion.arrives_ref, s32[4]{0:T(128)} %get-tuple-element.25.lengths_ref, bf16[64,128,256]{2,1,0:T(8,128)(2,1)} %copy-done, f32[4,2,256]{2,1,0:T(2,128)} %copy-done.1), custom_call_target="tpu_custom_call" | custom-call | tf_op jit(solution)/shard_map/place_pages/pallas_call | solution.py:713
  (7 shorter events, 0.1 us)
Async XLA Ops:
  122.7 1.9 %copy-start = (bf16[64,128,256]{2,1,0:T(8,128)(2,1)}, bf16[64,128,256]{2,1,0:T(8,128)(2,1)S(1)}, u32[]{:S(2)}) copy-start(bf16[64,128,256]{2,1,0:T(8,128)(2,1)S(1)} %get-tuple-element.6.arrived_ref) | copy-start | bytes 12582916
  124.7 0.6 copy-start.1

commit v3 on v2

--- a/solution.py
+++ b/solution.py
@@ -224,6 +224,10 @@
     )
     send_left = send_lengths - (send_ids % per_unit) * PAGE
     send_query = (send_units % KVH) * requests + send_units // KVH
+    own_lengths = pick(
+        (own_units // KVH)[:, None] == jnp.arange(requests, dtype=jnp.int32)[None, :],
+        context_lengths,
+    )
     own_heads, own_requests = own_units % KVH, own_units // KVH
     table = jnp.concatenate(
         [
@@ -231,30 +235,22 @@
             own_heads * requests + own_requests, own_heads, own_requests,
         ]
     )
-    return send_order, arrives_at, table
-
-
-def sort_kernel(order_ref, pages_ref, out_ref, buf, in_sem, out_sem):
-    count = buf.shape[0]
-
-    def inward(i):
-        return pltpu.make_async_copy(pages_ref.at[order_ref[i]], buf.at[i], in_sem.at[i])
-
-    def outward(i):
-        return pltpu.make_async_copy(buf.at[i], out_ref.at[i], out_sem.at[i])
+    return send_order, arrives_at, own_lengths, table
+
+
+def sort_kernel(order_ref, pages_ref, out_ref, sem):
+    count = out_ref.shape[0]
+
+    def move(i):
+        return pltpu.make_async_copy(pages_ref.at[order_ref[i]], out_ref.at[i], sem.at[i])
 
     @pl.loop(0, count)
     def _(i):
-        inward(i).start()
+        move(i).start()
 
     @pl.loop(0, count)
     def _(i):
-        inward(i).wait()
-        outward(i).start()
-
-    @pl.loop(0, count)
-    def _(i):
-        outward(i).wait()
+        move(i).wait()
 
 
 def place_kernel(arrives_ref, lengths_ref, arrived_ref, fresh_ref, out_ref, buf, in_sem, out_sem):
@@ -426,6 +422,7 @@
         load.start()
     pl.semaphore_wait(barrier, devices - 1)
     send_pages(0)
+    send_pages(1)
 
     for c in range(heads):
         loads[c].wait()
@@ -442,7 +439,7 @@
     def _(offset):
         row_copy(0, offset, me, near(offset)).start()
 
-    send_pages(1)
+    send_pages(2)
     for load in loads[heads + 1 :]:
         load.start()
     loads[heads].wait()
@@ -459,7 +456,7 @@
     def _(offset):
         row_copy(1, offset, partner, near(offset)).start()
 
-    send_pages(2)
+    send_pages(3)
 
     @pl.loop(1, half)
     def _(offset):
@@ -511,7 +508,7 @@
     def _(offset):
         part_copy(offset, lax.rem(here + offset, half), here, near(offset)).start()
 
-    send_pages(3)
+    send_pages(4)
 
     own_sums, own_totals = [], []
     row = lax.broadcasted_iota(jnp.int32, (2 * group_count, rows), 0)
@@ -558,7 +555,7 @@
     swap_out[U_DEV] = pack_totals([unpack_total(away[U_DEV], j) for j in range(U_DEV)])
     kept = half_sum(side)
     swap_copy().start()
-    send_pages(4)
+    send_pages(5)
     swap_copy().wait_recv()
     packed = kept[U_DEV] + swap_in[U_DEV].astype(jnp.float32)
     for j in range(U_DEV):
@@ -572,14 +569,14 @@
     def _(offset):
         att_copy(0, offset, me, near(offset)).start()
 
-    send_pages(5)
+    send_pages(6)
     att_copy(0, 0, partner, partner).wait_recv()
 
     @pl.loop(1, half)
     def _(offset):
         att_copy(1, offset, partner, near(offset)).start()
 
-    for batch in range(6, batches):
+    for batch in range(7, batches):
         send_pages(batch)
 
     @pl.loop(1, half)
@@ -645,7 +642,7 @@
     vmem = pl.BlockSpec(memory_space=pltpu.VMEM)
     smem = pl.BlockSpec(memory_space=pltpu.SMEM)
     dma = pltpu.SemaphoreType.DMA
-    send_order, arrives_at, table = index_tables(
+    send_order, arrives_at, own_lengths, table = index_tables(
         context_lengths, new_units, old_pages, pages_dev
     )
     positions = (
@@ -658,6 +655,7 @@
     cosine = jnp.concatenate([cosine, cosine], axis=-1)
     sine = jnp.concatenate([-sine, sine], axis=-1)
 
+    small_limit = 2 * cache_pages.size * cache_pages.dtype.itemsize
     buffers = [
         pltpu.VMEM(cache_pages.shape, jnp.bfloat16), dma((pages_dev,)), dma((pages_dev,)),
     ]
@@ -665,8 +663,9 @@
         sort_kernel,
         out_shape=jax.ShapeDtypeStruct(cache_pages.shape, jnp.bfloat16),
         in_specs=[smem, hbm],
-        out_specs=hbm,
-        scratch_shapes=buffers,
+        out_specs=vmem,
+        scratch_shapes=[dma((pages_dev,))],
+        compiler_params=pltpu.CompilerParams(vmem_limit_bytes=small_limit),
         name="sort_pages",
     )(send_order, cache_pages)
     tile = (2 * group_count, HD)
@@ -706,16 +705,13 @@
         ),
         name="layer",
     )(table, hidden_states.reshape(rows, D), cosine, sine, qkv_weight, out_weight, outgoing)
-    own_lengths = jnp.take(
-        context_lengths,
-        lax.dynamic_slice_in_dim(new_units, lax.axis_index("tp") * U_DEV, U_DEV) // KVH,
-    )
     placed = pl.pallas_call(
         place_kernel,
         out_shape=jax.ShapeDtypeStruct(cache_pages.shape, jnp.bfloat16),
         in_specs=[smem, smem, hbm, vmem],
         out_specs=hbm,
         scratch_shapes=buffers,
+        compiler_params=pltpu.CompilerParams(vmem_limit_bytes=small_limit),
         name="place_pages",
     )(arrives_at, own_lengths, arrived, fresh)
     return (mixed.reshape(requests, 2, out_weight.shape[0]), placed)

time: 132 us -> 143 us (1.083)
  Pallas kernels: 118 us -> 125 us
  local copies, waits for them, and re-layouts: 5.72 us -> 10.3 us
    unnamed x4 -> x8, local copies, waits for them, and re-layouts: 2.51 us -> 8.39 us
    pallas_call x1, Pallas kernels: 6.11 us -> 11.2 us  [fused_body(): pl.pallas_call(place_kernel, out_shape=jax.ShapeDtypeStruct(cache_pages.s...]
    pallas_call x1, Pallas kernels: 5.83 us -> 7.47 us  [fused_body(): pl.pallas_call(sort_kernel, out_shape=jax.ShapeDtypeStruct(cache_pages.sh...]
    reduce_sum x4 -> x5, other arithmetic: 3.09 us -> 3.45 us  [pick(): return jnp.sum(jnp.where(hit, values[None, :], 0), axis=1)]
where the time goes in v3:
time: 143 us
  Pallas kernels  125 us (87%)
  local copies, waits for them, and re-layouts  10.3 us (7%)
  other arithmetic  7.13 us (5%)
    pallas_call x1, Pallas kernels, fused_body(): pl.pallas_call(lambda *refs: layer_kernel(devices, capacity, *refs), out_...  106 us
    pallas_call x1, Pallas kernels, fused_body(): pl.pallas_call(place_kernel, out_shape=jax.ShapeDtypeStruct(cache_pages.s...  11.2 us
    unnamed x8, local copies, waits for them, and re-layouts  8.39 us
    pallas_call x1, Pallas kernels, fused_body(): pl.pallas_call(sort_kernel, out_shape=jax.ShapeDtypeStruct(cache_pages.sh...  7.47 us
    reduce_sum x5, other arithmetic, pick(): return jnp.sum(jnp.where(hit, values[None, :], 0), axis=1)  3.45 us

profile of v3, /device:TPU:1, one launch (start us, length us, event | category | flops | bytes accessed | tf_op | source)
XLA Modules:
  0.0 142.9 jit_solution(5567667776819088193)
XLA Ops:
  0.6 0.8 and_select_fusion.9
  1.4 0.8 select_reduce_fusion.2
  2.3 0.2 convert_reduce_fusion.1
  2.5 0.2 select_reduce_fusion.1
  2.7 0.7 select_reduce_fusion.6
  3.4 0.7 broadcast_multiply_fusion
  4.1 0.7 multiply_add_fusion.1
  4.9 0.1 concatenate.9.refs_0_
  5.0 0.8 select_reduce_fusion.7.lengths_ref
  5.8 0.1 iota_add_fusion
  5.9 0.1 add.133
  5.9 0.9 select_reduce_fusion
  6.9 0.2 convert_reduce_fusion
  7.1 0.7 add_convert_fusion
  7.8 0.1 convert_element_type.18
  7.9 0.1 fusion.1
  8.0 0.1 pad_maximum_fusion
  8.1 1.1 reshape.175.refs_1_
  9.1 0.0 copy-start.3
  9.1 2.2 %copy-done.3 = bf16[64,128,256]{2,1,0:T(8,128)(2,1)S(1)} copy-done((bf16[64,128,256]{2,1,0:T(8,128)(2,1)S(1)}, bf16[64,128,256]{2,1,0:T(8,128)(2,1)}, u32[]{:S(2)}) %copy-start.3) | copy-done | bytes 4194328
  11.3 7.5 %sort_pages.1.refs_6_ = bf16[64,128,256]{2,1,0:T(8,128)(2,1)S(1)} custom-call(s32[64]{0:T(128)S(1)} %get-tuple-element.8.order_ref, bf16[64,128,256]{2,1,0:T(8,128)(2,1)S(1)} %copy-done.3), custom_call_target="tpu_custom_call" | custom-call | tf_op jit(solution)/shard_map/sort_pages/pallas_call | solution.py:662
  18.8 0.0 copy-start
  18.8 2.0 %copy-done = bf16[64,128,256]{2,1,0:T(8,128)(2,1)} copy-done((bf16[64,128,256]{2,1,0:T(8,128)(2,1)}, bf16[64,128,256]{2,1,0:T(8,128)(2,1)S(1)}, u32[]{:S(2)}) %copy-start) | copy-done | bytes 4194328
  20.8 106.1 %layer.1 = (bf16[64,128,256]{2,1,0:T(8,128)(2,1)S(1)}, bf16[16,512]{1,0:T(8,128)(2,1)S(1)}, f32[4,2,256]{2,1,0:T(2,128)S(1)}) custom-call(s32[268]{0:T(512)S(1)} %concatenate.9.refs_0_, bf16[16,8192]{1,0:T(8,128)(2,1)S(1)} %reshape.175.refs_1_, f32[16,128]{1,0:T(8,128)S(1)} %get-tuple-element.27.refs_2_, f32[16,128]{1,0:T(8,128)S(1)} %get-tuple-element.28.refs_3_, ...), custom_call_target="tpu_custom_call" | custom-call | tf_op jit(solution)/shard_map/layer/pallas_call | solution.py:672
  126.9 0.0 copy-start.1
  126.9 2.0 %copy-done.1 = bf16[64,128,256]{2,1,0:T(8,128)(2,1)} copy-done((bf16[64,128,256]{2,1,0:T(8,128)(2,1)}, bf16[64,128,256]{2,1,0:T(8,128)(2,1)S(1)}, u32[]{:S(2)}) %copy-start.1) | copy-done | bytes 4194328
  128.9 0.6 reshape.176
  129.5 0.0 copy-start.2
  129.5 2.2 %copy-done.2 = bf16[64,128,256]{2,1,0:T(8,128)(2,1)S(1)} copy-done((bf16[64,128,256]{2,1,0:T(8,128)(2,1)S(1)}, bf16[64,128,256]{2,1,0:T(8,128)(2,1)}, u32[]{:S(2)}) %copy-start.2) | copy-done | bytes 4194328
  131.7 11.2 %place_pages.1 = bf16[64,128,256]{2,1,0:T(8,128)(2,1)} custom-call(s32[64]{0:T(128)S(1)} %multiply_add_fusion.arrives_ref, s32[4]{0:T(128)S(1)} %select_reduce_fusion.7.lengths_ref, bf16[64,128,256]{2,1,0:T(8,128)(2,1)S(1)} %copy-done.2, f32[4,2,256]{2,1,0:T(2,128)S(1)} %get-tuple-element.7.fresh_ref), custom_call_target="tpu_custom_call" | custom-call | tf_op jit(solution)/shard_map/place_pages/pallas_call | solution.py:708
  (7 shorter events, 0.1 us)
Async XLA Ops:
  9.1 2.2 %copy-start.3 = (bf16[64,128,256]{2,1,0:T(8,128)(2,1)S(1)}, bf16[64,128,256]{2,1,0:T(8,128)(2,1)}, u32[]{:S(2)}) copy-start(bf16[64,128,256]{2,1,0:T(8,128)(2,1)} %pages_ref.1) | copy-start | bytes 12582916
  18.8 2.0 %copy-start = (bf16[64,128,256]{2,1,0:T(8,128)(2,1)}, bf16[64,128,256]{2,1,0:T(8,128)(2,1)S(1)}, u32[]{:S(2)}) copy-start(bf16[64,128,256]{2,1,0:T(8,128)(2,1)S(1)} %sort_pages.1.refs_6_) | copy-start | bytes 12582916
  126.9 2.0 %copy-start.1 = (bf16[64,128,256]{2,1,0:T(8,128)(2,1)}, bf16[64,128,256]{2,1,0:T(8,128)(2,1)S(1)}, u32[]{:S(2)}) copy-start(bf16[64,128,256]{2,1,0:T(8,128)(2,1)S(1)} %get-tuple-element.6.arrived_ref) | copy-start | bytes 12582916
  129.5 2.2 %copy-start.2 = (bf16[64,128,256]{2,1,0:T(8,128)(2,1)S(1)}, bf16[64,128,256]{2,1,0:T(8,128)(2,1)}, u32[]{:S(2)}) copy-start(bf16[64,128,256]{2,1,0:T(8,128)(2,1)} %copy-done.1) | copy-start | bytes 12582916

commit v4 on v3

--- a/solution.py
+++ b/solution.py
@@ -238,19 +238,27 @@
     return send_order, arrives_at, own_lengths, table
 
 
-def sort_kernel(order_ref, pages_ref, out_ref, sem):
-    count = out_ref.shape[0]
-
-    def move(i):
-        return pltpu.make_async_copy(pages_ref.at[order_ref[i]], out_ref.at[i], sem.at[i])
+def sort_kernel(order_ref, pages_ref, out_ref, buf, in_sem, out_sem):
+    count = buf.shape[0]
+
+    def inward(i):
+        return pltpu.make_async_copy(pages_ref.at[order_ref[i]], buf.at[i], in_sem.at[i])
+
+    def outward(i):
+        return pltpu.make_async_copy(buf.at[i], out_ref.at[i], out_sem.at[i])
 
     @pl.loop(0, count)
     def _(i):
-        move(i).start()
+        inward(i).start()
 
     @pl.loop(0, count)
     def _(i):
-        move(i).wait()
+        inward(i).wait()
+        outward(i).start()
+
+    @pl.loop(0, count)
+    def _(i):
+        outward(i).wait()
 
 
 def place_kernel(arrives_ref, lengths_ref, arrived_ref, fresh_ref, out_ref, buf, in_sem, out_sem):
@@ -638,7 +646,7 @@
     tiles = out_weight.shape[0] // HD
     group_count = HEADS // KVH
     units = new_units.shape[0]
-    hbm = pl.BlockSpec(memory_space=pl.ANY)
+    hbm = pl.BlockSpec(memory_space=pltpu.HBM)
     vmem = pl.BlockSpec(memory_space=pltpu.VMEM)
     smem = pl.BlockSpec(memory_space=pltpu.SMEM)
     dma = pltpu.SemaphoreType.DMA
@@ -655,7 +663,6 @@
     cosine = jnp.concatenate([cosine, cosine], axis=-1)
     sine = jnp.concatenate([-sine, sine], axis=-1)
 
-    small_limit = 2 * cache_pages.size * cache_pages.dtype.itemsize
     buffers = [
         pltpu.VMEM(cache_pages.shape, jnp.bfloat16), dma((pages_dev,)), dma((pages_dev,)),
     ]
@@ -663,9 +670,8 @@
         sort_kernel,
         out_shape=jax.ShapeDtypeStruct(cache_pages.shape, jnp.bfloat16),
         in_specs=[smem, hbm],
-        out_specs=vmem,
-        scratch_shapes=[dma((pages_dev,))],
-        compiler_params=pltpu.CompilerParams(vmem_limit_bytes=small_limit),
+        out_specs=hbm,
+        scratch_shapes=buffers,
         name="sort_pages",
     )(send_order, cache_pages)
     tile = (2 * group_count, HD)
@@ -701,7 +707,7 @@
             dma(()),
         ],
         compiler_params=pltpu.CompilerParams(
-            collective_id=0, has_side_effects=True, vmem_limit_bytes=48 << 20
+            collective_id=0, has_side_effects=True, vmem_limit_bytes=61 << 20
         ),
         name="layer",
     )(table, hidden_states.reshape(rows, D), cosine, sine, qkv_weight, out_weight, outgoing)
@@ -711,7 +717,6 @@
         in_specs=[smem, smem, hbm, vmem],
         out_specs=hbm,
         scratch_shapes=buffers,
-        compiler_params=pltpu.CompilerParams(vmem_limit_bytes=small_limit),
         name="place_pages",
     )(arrives_at, own_lengths, arrived, fresh)
     return (mixed.reshape(requests, 2, out_weight.shape[0]), placed)

time: 143 us -> 133 us (0.930)
  local copies, waits for them, and re-layouts: 10.3 us -> 3.89 us
  Pallas kernels: 125 us -> 119 us
  other arithmetic: 7.13 us -> 9.33 us
    unnamed x8 -> x0, local copies, waits for them, and re-layouts: 8.39 us -> none
    pallas_call x1, Pallas kernels: 11.2 us -> 5.98 us  [fused_body(): pl.pallas_call(place_kernel, out_shape=jax.ShapeDtypeStruct(cache_pages.s...]
    pallas_call x1, Pallas kernels: 7.47 us -> 5.83 us  [fused_body(): pl.pallas_call(sort_kernel, out_shape=jax.ShapeDtypeStruct(cache_pages.sh...]
where the time goes in v4:
time: 133 us
  Pallas kernels  119 us (89%)
  other arithmetic  9.33 us (7%)
  local copies, waits for them, and re-layouts  3.89 us (3%)
    pallas_call x1, Pallas kernels, fused_body(): pl.pallas_call(lambda *refs: layer_kernel(devices, capacity, *refs), out_...  107 us
    pallas_call x1, Pallas kernels, fused_body(): pl.pallas_call(place_kernel, out_shape=jax.ShapeDtypeStruct(cache_pages.s...  5.98 us
    pallas_call x1, Pallas kernels, fused_body(): pl.pallas_call(sort_kernel, out_shape=jax.ShapeDtypeStruct(cache_pages.sh...  5.83 us
    reduce_sum x5, other arithmetic, pick(): return jnp.sum(jnp.where(hit, values[None, :], 0), axis=1)  4.51 us

profile of v4, /device:TPU:1, one launch (start us, length us, event | category | flops | bytes accessed | tf_op | source)
XLA Modules:
  0.0 132.9 jit_solution(6862333816300413397)
XLA Ops:
  0.6 0.8 and_select_fusion.9
  1.4 0.8 select_reduce_fusion.2
  2.3 0.2 convert_reduce_fusion.1
  2.5 0.6 select_reduce_fusion.1
  3.1 0.7 select_reduce_fusion.6
  3.9 0.7 broadcast_multiply_fusion
  4.6 0.7 multiply_add_fusion.1
  5.4 0.7 concatenate.9.refs_0_
  6.0 1.4 %select_reduce_fusion.7.lengths_ref = s32[4]{0:T(128)} fusion(s32[8]{0:T(128)} %param.11, s32[4]{0:T(128)S(1)} %get-tuple-element.15), kind=kLoop, calls=%fused_computation.20 | loop fusion | flops 92 | bytes 64 | tf_op jit(solution)/shard_map/reduce_sum | solution.py:195
  7.4 0.1 iota_add_fusion
  7.5 0.1 add.133
  7.6 0.9 select_reduce_fusion
  8.5 0.2 convert_reduce_fusion
  8.7 0.6 multiply_add_fusion.arrives_ref
  9.2 0.7 add_convert_fusion
  10.0 0.1 convert_element_type.18
  10.0 0.1 fusion.1
  10.2 0.7 pad_maximum_fusion
  10.8 1.7 %reshape.175.refs_1_ = bf16[16,8192]{1,0:T(8,128)(2,1)} reshape(bf16[8,2,8192]{2,1,0:T(2,128)(2,1)} %param.7) | data formatting | bytes 524288 | tf_op jit(solution)/shard_map/reshape | solution.py:713
  12.6 5.8 %sort_pages.1.refs_6_ = bf16[64,128,256]{2,1,0:T(8,128)(2,1)} custom-call(s32[64]{0:T(128)} %get-tuple-element.8.order_ref, bf16[64,128,256]{2,1,0:T(8,128)(2,1)} %pages_ref.1), custom_call_target="tpu_custom_call" | custom-call | tf_op jit(solution)/shard_map/sort_pages/pallas_call | solution.py:669
  18.4 107.2 %layer.1 = (bf16[64,128,256]{2,1,0:T(8,128)(2,1)}, bf16[16,512]{1,0:T(8,128)(2,1)}, f32[4,2,256]{2,1,0:T(2,128)}) custom-call(s32[268]{0:T(512)} %concatenate.9.refs_0_, bf16[16,8192]{1,0:T(8,128)(2,1)} %reshape.175.refs_1_, f32[16,128]{1,0:T(8,128)} %get-tuple-element.27.refs_2_, f32[16,128]{1,0:T(8,128)} %get-tuple-element.28.refs_3_, ...), custom_call_target="tpu_custom_call" | custom-call | tf_op jit(solution)/shard_map/layer/pallas_call | solution.py:678
  125.6 1.3 %reshape.176 = bf16[8,2,512]{2,1,0:T(2,128)(2,1)} reshape(bf16[16,512]{1,0:T(8,128)(2,1)} %get-tuple-element.5) | data formatting | bytes 32768 | tf_op jit(solution)/shard_map/reshape | solution.py:722
  127.0 6.0 %place_pages.1 = bf16[64,128,256]{2,1,0:T(8,128)(2,1)} custom-call(s32[64]{0:T(128)} %multiply_add_fusion.arrives_ref, s32[4]{0:T(128)} %select_reduce_fusion.7.lengths_ref, bf16[64,128,256]{2,1,0:T(8,128)(2,1)} %get-tuple-element.6.arrived_ref, f32[4,2,256]{2,1,0:T(2,128)} %get-tuple-element.7.fresh_ref), custom_call_target="tpu_custom_call" | custom-call | tf_op jit(solution)/shard_map/place_pages/pallas_call | solution.py:714
  (6 shorter events, 0.1 us)
